TPU v7x, 512 devices: a whole 4x8x8 slice. The times are simulated.
512 devices in a mesh: vox: 32 (over x, z), smp: 16 (over y, core).
Axes of the slice: x: 4, y: 8, z: 8, core: 2. Of those that a mesh axis runs over, the one named last changes fastest.
Arguments:
- ensemble: float32 [4096, 128, 128], P('vox', 'smp'), may hold values from -6 to 6
- voxel_factor: float32 [4096, 128], P('vox'), may hold values from -6 to 6
- sample_factor: float32 [128, 128], P('smp'), may hold values from -6 to 6
- time_factor: float32 [128, 128], replicated, may hold values from -6 to 6
- weights: float32 [128], replicated, may hold values from 0.005 to 0.02
Outputs:
- voxel_result: float32 [4096, 128], P('vox')
- sample_result: float32 [128, 128], P('smp')
- time_result: float32 [128, 128], replicated
- scale_result: float32 [128], replicated
All inputs are finite; a program needn't handle non-finite values. Where the computation divides by a largest or mean magnitude, that divisor is 1e-20 or more.
Results may differ from a plain program's by a relative error of at most 0.0001.
Values sent between devices are 32-bit elements; how exact they have to be, the bound alone decides.
A program may use at most 64 MiB of HBM per device.

v0:
```python
import jax
import jax.numpy as jnp
from jax import lax
from jax.sharding import PartitionSpec as P

HIGH = lax.Precision.HIGHEST


def descend(factor, terms, hadamard, weights):
    coupled = weights[:, None] * weights[None, :] * hadamard
    step_size = 1.0 / jnp.max(jnp.sum(jnp.abs(coupled), axis=1))
    product = jnp.dot(factor, coupled, precision=HIGH, preferred_element_type=jnp.float32)
    return factor - step_size * (product - terms * weights[None, :])


def rescale(moved, gram, row_count):
    scales = jnp.sqrt(jnp.diagonal(gram) / row_count + 1e-06)
    return (moved / scales[None, :], gram / (scales[:, None] * scales[None, :]), scales)


def local_gram(moved):
    return jnp.dot(moved.T, moved, precision=HIGH, preferred_element_type=jnp.float32)


def per_device(ensemble, voxel_factor, sample_factor, time_factor, weights):
    vox_rows, smp_rows, time_count = ensemble.shape
    rank_count = voxel_factor.shape[1]
    voxel_total = vox_rows * lax.axis_size("vox")
    sample_total = smp_rows * lax.axis_size("smp")
    flat = ensemble.reshape(vox_rows * smp_rows, time_count)
    gram_b = lax.psum(local_gram(sample_factor), "smp")
    gram_c = local_gram(time_factor)
    contracted = jnp.dot(flat, time_factor, precision=HIGH, preferred_element_type=jnp.float32)
    contracted = contracted.reshape(vox_rows, smp_rows, rank_count)
    partial_value = jnp.einsum("ijr,jr->ir", contracted, sample_factor, precision=HIGH)
    terms_a = lax.psum(partial_value, "smp")
    moved = descend(voxel_factor, terms_a, gram_b * gram_c, weights)
    gram = lax.psum(local_gram(moved), "vox")
    voxel_factor, gram_a, scales = rescale(moved, gram, voxel_total)
    partial_b = jnp.einsum("ijr,ir->jr", contracted, voxel_factor, precision=HIGH)
    terms_b = lax.psum(partial_b, "vox")
    weights = weights * scales
    moved = descend(sample_factor, terms_b, gram_a * gram_c, weights)
    gram = lax.psum(local_gram(moved), "smp")
    sample_factor, gram_b, scales = rescale(moved, gram, sample_total)
    paired = (voxel_factor[:, None, :] * sample_factor[None, :, :]).reshape(
        vox_rows * smp_rows, rank_count
    )
    partial_c = jnp.einsum("nk,nr->kr", flat, paired, precision=HIGH)
    terms_c = lax.psum(partial_c, ("vox", "smp"))
    weights = weights * scales
    moved = descend(time_factor, terms_c, gram_a * gram_b, weights)
    time_factor, gram_c, scales = rescale(moved, local_gram(moved), time_count)
    weights = weights * scales
    return (voxel_factor, sample_factor, time_factor, weights)


def solution(mesh):
    return jax.shard_map(
        per_device,
        mesh=mesh,
        in_specs=(P("vox", "smp", None), P("vox", None), P("smp", None), P(), P()),
        out_specs=(P("vox", None), P("smp", None), P(), P()),
        check_vma=False,
    )
```

profile of v0, /device:TPU:1, one launch (start us, length us, event | category | flops | bytes accessed | tf_op | source)
XLA Modules:
  0.0 745.5 jit_solution(5589847889184685163)
XLA Ops:
  7.2 0.0 copy-start.3
  7.2 0.0 all-reduce.12.cloned.1.call-start
  7.2 1.7 fusion.19
  8.9 0.0 copy-done.3
  8.9 2.2 multiply_reduce_fusion.1
  11.2 0.0 all-reduce.12.cloned.1.call-update
  11.2 0.0 copy-start.10
  11.2 0.0 all-reduce.6.cloned.1.call-start
  11.3 120.5 %all-reduce.12.cloned.1.call-done = (f32[128,128]{1,0:T(8,128)}, f32[128,128]{1,0:T(8,128)}) async-done(((f32[128,128]{1,0:T(8,128)}, f32[128,128]{1,0:T(8,128)}), (f32[128,128]{1,0:T(8,128)}, f32[128,128]{1,0:T(8,128)})) %all-reduce.12.cloned.1.call-update) | async-done | bytes 131088 | tf_op jit(solution)/shard_map/psum | solution.py:36
  131.8 0.0 copy-done.10
  131.8 1.3 abs_reduce_fusion.2
  133.1 0.6 reduce_max.27
  134.4 0.0 copy-done.5
  134.4 0.0 copy-done.7
  134.4 0.0 copy-done.8
  134.4 0.3 fusion.5
  134.7 0.9 fusion.20
  135.6 0.0 all-reduce.6.cloned.1.call-update
  135.7 0.0 all-reduce.8.cloned.1.call-start
  135.7 149.7 %all-reduce.6.cloned.1.call-done = f32[128,128]{1,0:T(8,128)} async-done(((f32[128,128]{1,0:T(8,128)}), f32[128,128]{1,0:T(8,128)}) %all-reduce.6.cloned.1.call-update) | async-done | bytes 65552 | tf_op jit(solution)/shard_map/psum | solution.py:38
  285.5 2.0 gather_fusion
  287.5 0.0 copy-done
  287.5 0.2 abs_reduce_fusion.1
  287.7 0.0 copy-start.4
  287.8 0.0 copy-start.2
  287.8 58.8 %psum.45 = f32[8,128]{1,0:T(8,128)S(1)} all-reduce(f32[8,128]{1,0:T(8,128)S(1)} %bitcast.61), channel_id=1, replica_groups=mesh['vox'=32,'smp'=16] {'vox'}, use_global_device_ids=true, to_apply=%region_7.8 | all-reduce | flops 1024 | bytes 8192 | tf_op jit(solution)/shard_map/psum | solution.py:41
  346.6 0.6 reduce_max.28
  347.9 0.2 fusion.8
  348.0 0.9 fusion.21
  349.0 0.0 all-reduce.8.cloned.1.call-update
  349.0 0.0 all-reduce.10.cloned.1.call-start
  349.0 0.0 copy-done.4
  349.1 0.1 copy.22
  349.1 118.5 %all-reduce.8.cloned.1.call-done = f32[128,128]{1,0:T(8,128)} async-done(((f32[128,128]{1,0:T(8,128)}), f32[128,128]{1,0:T(8,128)}) %all-reduce.8.cloned.1.call-update) | async-done | bytes 65552 | tf_op jit(solution)/shard_map/psum | solution.py:44
  467.6 1.9 gather_fusion.1
  469.6 0.0 copy-start.9
  469.6 1.8 convolution_bitcast_fusion
  471.4 0.0 copy-done.9
  471.4 0.0 all-reduce.10.cloned.1.call-update
  471.4 0.8 copy-done.1
  472.2 0.2 abs_reduce_fusion
  472.4 0.6 reduce_max.29
  473.7 261.4 %all-reduce.10.cloned.1.call-done = f32[128,128]{1,0:T(8,128)} async-done(((f32[128,128]{1,0:T(8,128)}), f32[128,128]{1,0:T(8,128)}) %all-reduce.10.cloned.1.call-update) | async-done | bytes 65552 | tf_op jit(solution)/shard_map/psum | solution.py:50
  735.2 1.0 fusion.2
  736.2 0.3 fusion.22
  736.5 1.2 gather_fusion.2
  737.8 0.5 fusion.18
  738.3 0.6 broadcast_divide_fusion
  (13 shorter events, 0.1 us)
Async XLA Ops:
  7.2 1.8 copy-start.3
  7.2 124.6 %all-reduce.12.cloned.1.call-start = ((), (), s32[]{:S(2)}) async-start(), calls=%async_computation.3 | async-start | bytes 262144 | tf_op jit(solution)/shard_map/psum | solution.py:36
  7.2 1.7 copy-start.6
  11.2 120.6 %copy-start.10 = (f32[128]{0:T(128)S(1)}, f32[128]{0:T(128)}, u32[]{:S(2)}) copy-start(f32[128]{0:T(128)} %param.9) | copy-start | bytes 1540
  11.2 274.2 %all-reduce.6.cloned.1.call-start = ((), (), s32[]{:S(2)}) async-start(), calls=%async_computation | async-start | bytes 131072 | tf_op jit(solution)/shard_map/psum | solution.py:38
  131.8 2.6 copy-start.5
  131.8 2.6 copy-start.7
  131.8 2.6 copy-start.8
  135.7 332.0 %all-reduce.8.cloned.1.call-start = ((), (), s32[]{:S(2)}) async-start(), calls=%async_computation.1 | async-start | bytes 131072 | tf_op jit(solution)/shard_map/psum | solution.py:44
  285.5 2.0 copy-start
  287.7 61.4 %copy-start.4 = (f32[128,128]{1,0:T(8,128)}, f32[128,128]{1,0:T(8,128)S(1)}, u32[]{:S(2)}) copy-start(f32[128,128]{1,0:T(8,128)S(1)} %get-tuple-element.14) | copy-start | bytes 196612
  287.8 181.8 %copy-start.2 = (f32[128,8,128]{2,1,0:T(8,128)S(1)}, f32[128,8,128]{2,1,0:T(8,128)}, u32[]{:S(2)}) copy-start(f32[128,8,128]{2,1,0:T(8,128)} %param.5) | copy-start | bytes 1572868
  349.0 386.2 %all-reduce.10.cloned.1.call-start = ((), (), s32[]{:S(2)}) async-start(), calls=%async_computation.2 | async-start | bytes 131072 | tf_op jit(solution)/shard_map/psum | solution.py:50
  469.6 1.8 copy-start.9
  471.4 0.8 copy-start.1
Sparse Core Ops, SparseCore 0:
  11.3 120.4 all-reduce.11
  135.8 149.5 all-reduce.5
  349.1 118.4 all-reduce.7
  473.0 262.0 all-reduce.9
where the time goes:
time: 746 us; the launch traced here: 745 us
  waiting for transfers between devices  650 us (87%)
  blocking collectives  58.8 us (8%)
  between operations  16 us (2%)
  matrix products  10.6 us (1%)
    psum x1, waiting for transfers between devices, per_device(): terms_c = lax.psum(partial_c, ('vox', 'smp'))  261 us
    psum x1, waiting for transfers between devices, per_device(): gram = lax.psum(local_gram(moved), 'vox')  150 us
    psum x1, waiting for transfers between devices, per_device(): terms_a = lax.psum(partial_value, 'smp')  121 us
    psum x1, waiting for transfers between devices, per_device(): gram = lax.psum(local_gram(moved), 'smp')  118 us
    psum x1, blocking collectives, per_device(): terms_b = lax.psum(partial_b, 'vox')  58.8 us
  transfers between devices with their start and end apart: 4, of which 4 were waited for; matrix products, arithmetic and copies ran while one was open for 0% of the time, Pallas kernels for 0%

commit v1 on v0

--- a/solution.py
+++ b/solution.py
@@ -35,7 +35,7 @@
     partial_value = jnp.einsum("ijr,jr->ir", contracted, sample_factor, precision=HIGH)
     terms_a = lax.psum(partial_value, "smp")
     moved = descend(voxel_factor, terms_a, gram_b * gram_c, weights)
-    gram = lax.psum(local_gram(moved), "vox")
+    gram = jnp.sum(lax.all_gather(local_gram(moved), "vox"), axis=0)
     voxel_factor, gram_a, scales = rescale(moved, gram, voxel_total)
     partial_b = jnp.einsum("ijr,ir->jr", contracted, voxel_factor, precision=HIGH)
     terms_b = lax.psum(partial_b, "vox")

time: 746 us -> 678 us (0.909)
  waiting for transfers between devices: 650 us -> 580 us
    psum x1 -> x0, waiting for transfers between devices: 150 us -> none  [per_device(): gram = lax.psum(local_gram(moved), 'vox')]
    all_gather x0 -> x1, waiting for transfers between devices: none -> 80.1 us  [per_device(): gram = jnp.sum(lax.all_gather(local_gram(moved), 'vox'), axis=0)]
where the time goes in v1:
time: 678 us
  waiting for transfers between devices  580 us (86%)
  blocking collectives  58.7 us (9%)
  between operations  16 us (2%)
  matrix products  11.6 us (2%)
    psum x1, waiting for transfers between devices, per_device(): terms_c = lax.psum(partial_c, ('vox', 'smp'))  261 us
    psum x1, waiting for transfers between devices, per_device(): terms_a = lax.psum(partial_value, 'smp')  121 us
    psum x1, waiting for transfers between devices, per_device(): gram = lax.psum(local_gram(moved), 'smp')  118 us
    all_gather x1, waiting for transfers between devices, per_device(): gram = jnp.sum(lax.all_gather(local_gram(moved), 'vox'), axis=0)  80.1 us
    psum x1, blocking collectives, per_device(): terms_b = lax.psum(partial_b, 'vox')  58.7 us
  transfers between devices with their start and end apart: 4, of which 4 were waited for; matrix products, arithmetic and copies ran while one was open for 0% of the time, Pallas kernels for 0%

profile of v1, /device:TPU:1, one launch (start us, length us, event | category | flops | bytes accessed | tf_op | source)
XLA Modules:
  0.0 677.5 jit_solution(13857174595154442184)
XLA Ops:
  7.2 0.0 all-reduce.9.cloned.1.call-start
  7.2 1.7 fusion.19
  8.9 2.3 multiply_reduce_fusion.1
  11.2 0.0 copy-start.5
  11.2 0.0 all-reduce.9.cloned.1.call-update
  11.2 0.0 all-gather.3.cloned.1.call-start
  11.3 120.6 %all-reduce.9.cloned.1.call-done = (f32[128,128]{1,0:T(8,128)}, f32[128,128]{1,0:T(8,128)}) async-done(((f32[128,128]{1,0:T(8,128)}, f32[128,128]{1,0:T(8,128)}), (f32[128,128]{1,0:T(8,128)}, f32[128,128]{1,0:T(8,128)})) %all-reduce.9.cloned.1.call-update) | async-done | bytes 131088 | tf_op jit(solution)/shard_map/psum | solution.py:36
  131.8 1.3 abs_reduce_fusion.2
  133.1 0.6 reduce_max.27
  134.4 0.0 copy-start.3
  134.4 1.3 fusion.5
  135.7 0.9 fusion.20
  136.6 0.0 all-gather.3.cloned.1.call-update
  136.6 0.0 all-reduce.5.cloned.1.call-start
  136.7 80.1 %all-gather.3.cloned.1.call-done = f32[4096,128]{1,0:T(8,128)} async-done(((f32[128,128]{1,0:T(8,128)}), f32[4096,128]{1,0:T(8,128)}) %all-gather.3.cloned.1.call-update) | async-done | bytes 2097168 | tf_op jit(solution)/shard_map/all_gather | solution.py:38
  216.8 0.0 copy-start
  216.8 1.8 reduce_sum.37
  218.6 0.0 copy-start.1
  218.6 1.2 gather_fusion
  219.9 0.0 copy-done.5
  219.9 0.2 abs_reduce_fusion.1
  220.1 0.0 copy-start.2
  220.1 58.7 %psum.37 = f32[8,128]{1,0:T(8,128)S(1)} all-reduce(f32[8,128]{1,0:T(8,128)S(1)} %bitcast.63), channel_id=1, replica_groups=mesh['vox'=32,'smp'=16] {'vox'}, use_global_device_ids=true, to_apply=%region_7.8 | all-reduce | flops 1024 | bytes 8192 | tf_op jit(solution)/shard_map/psum | solution.py:41
  278.8 0.6 reduce_max.28
  280.1 0.0 copy-done.3
  280.1 0.2 fusion.8
  280.3 0.9 fusion.21
  281.2 0.0 all-reduce.5.cloned.1.call-update
  281.2 0.0 all-reduce.7.cloned.1.call-start
  281.3 0.1 copy.22
  281.4 118.3 %all-reduce.5.cloned.1.call-done = f32[128,128]{1,0:T(8,128)} async-done(((f32[128,128]{1,0:T(8,128)}), f32[128,128]{1,0:T(8,128)}) %all-reduce.5.cloned.1.call-update) | async-done | bytes 65552 | tf_op jit(solution)/shard_map/psum | solution.py:44
  399.7 1.9 gather_fusion.1
  401.6 0.0 copy-done
  401.6 0.0 copy-start.4
  401.6 1.8 convolution_bitcast_fusion
  403.4 0.0 all-reduce.7.cloned.1.call-update
  403.4 1.0 abs_reduce_fusion
  404.5 0.6 reduce_max.29
  405.8 261.4 %all-reduce.7.cloned.1.call-done = f32[128,128]{1,0:T(8,128)} async-done(((f32[128,128]{1,0:T(8,128)}), f32[128,128]{1,0:T(8,128)}) %all-reduce.7.cloned.1.call-update) | async-done | bytes 65552 | tf_op jit(solution)/shard_map/psum | solution.py:50
  667.2 0.0 copy-done.1
  667.2 1.0 fusion.2
  668.3 0.3 fusion.22
  668.6 1.2 gather_fusion.2
  669.8 0.5 fusion.18
  670.3 0.6 broadcast_divide_fusion
  671.0 0.0 copy-done.2
  671.0 0.0 copy-done.4
  (5 shorter events, 0.1 us)
Async XLA Ops:
  7.2 124.7 %all-reduce.9.cloned.1.call-start = ((), (), s32[]{:S(2)}) async-start(), calls=%async_computation.3 | async-start | bytes 262144 | tf_op jit(solution)/shard_map/psum | solution.py:36
  11.2 208.7 %copy-start.5 = (f32[128]{0:T(128)S(1)}, f32[128]{0:T(128)}, u32[]{:S(2)}) copy-start(f32[128]{0:T(128)} %param.9) | copy-start | bytes 1540
  11.2 205.6 %all-gather.3.cloned.1.call-start = ((), (), s32[]{:S(2)}) async-start(), calls=%async_computation.2 | async-start | bytes 2162688 | tf_op jit(solution)/shard_map/all_gather | solution.py:38
  134.4 145.7 %copy-start.3 = (f32[8,128]{1,0:T(8,128)S(1)}, f32[8,128]{1,0:T(8,128)}, u32[]{:S(2)}) copy-start(f32[8,128]{1,0:T(8,128)} %param.7) | copy-start | bytes 12292
  136.6 263.0 %all-reduce.5.cloned.1.call-start = ((), (), s32[]{:S(2)}) async-start(), calls=%async_computation | async-start | bytes 131072 | tf_op jit(solution)/shard_map/psum | solution.py:44
  216.8 184.8 %copy-start = (f32[128,8,128]{2,1,0:T(8,128)S(1)}, f32[128,8,128]{2,1,0:T(8,128)}, u32[]{:S(2)}) copy-start(f32[128,8,128]{2,1,0:T(8,128)} %param.5) | copy-start | bytes 1572868
  218.6 448.6 %copy-start.1 = (f32[128,128]{1,0:T(8,128)S(1)}, f32[128,128]{1,0:T(8,128)}, u32[]{:S(2)}) copy-start(f32[128,128]{1,0:T(8,128)} %param.8) | copy-start | bytes 196612
  220.1 450.9 %copy-start.2 = (f32[128,128]{1,0:T(8,128)}, f32[128,128]{1,0:T(8,128)S(1)}, u32[]{:S(2)}) copy-start(f32[128,128]{1,0:T(8,128)S(1)} %get-tuple-element.14) | copy-start | bytes 196612
  281.2 386.0 %all-reduce.7.cloned.1.call-start = ((), (), s32[]{:S(2)}) async-start(), calls=%async_computation.1 | async-start | bytes 131072 | tf_op jit(solution)/shard_map/psum | solution.py:50
  401.6 269.4 %copy-start.4 = (f32[8,128]{1,0:T(8,128)}, f32[8,128]{1,0:T(8,128)S(1)}, u32[]{:S(2)}) copy-start(f32[8,128]{1,0:T(8,128)S(1)} %broadcast_divide_fusion.2) | copy-start | bytes 12292
Sparse Core Ops, SparseCore 0:
  11.3 120.4 all-reduce.8
  136.7 80.0 all-gather.2
  281.3 118.2 all-reduce.4
  405.1 262.0 all-reduce.6
